TPU v7x, 512 devices: a whole 4x4x16 slice. The times are simulated.
512 devices in a mesh: frame: 16 (over z), dom: 8 (over x, core), coef: 4 (over y).
Axes of the slice: x: 4, y: 4, z: 16, core: 2. Of those that a mesh axis runs over, the one named last changes fastest.
Arguments:
- geometry: float32 [32, 524288], P('coef', ('frame', 'dom')), may hold values from -1 to 1
- fraction: float32 [32, 524288], P('coef', ('frame', 'dom')), may hold values from 0 to 1
- interval: int32 [32, 524288], P('coef', ('frame', 'dom')), may hold values from 0 to 156
- pattern: int32 [32, 4096], P('coef', ('frame', 'dom')), may hold values from 0 to 95
- target: float32 [524288], P(('frame', 'dom')), may hold values from -8 to 8
Outputs:
- solution: float32 [384, 160], P('coef')
- residual: float32 [524288], P(('frame', 'dom'))
Inputs may be any that keep to these rules, and one draw needn't show every extreme that they name: The spline of a slot reads coefficients interval to interval + 3 of its type. Slot s refers to pair type (s // 8) * 96 + pattern.
All inputs are finite; a program needn't handle non-finite values.
Results may differ from a plain program's by a relative error of at most 0.0003.
Values sent between devices are 32-bit elements; how exact they have to be, the bound alone decides.
No kernel may reach another device: no remote copies, remote signals or barrier semaphores. Data moves between devices by JAX's collectives and lax.ppermute only.
A program may use at most 64 MiB of HBM per device.

v0:
```python
import math
import jax
import jax.numpy as jnp
from jax import lax
from jax.sharding import PartitionSpec as P

NK = 160
TYPES = 384
ITERS = 2


def spline_weights(fraction):
    square = fraction * fraction
    cube = square * fraction
    return (
        (1.0 - fraction) ** 3 / 6.0,
        (3.0 * cube - 6.0 * square + 4.0) / 6.0,
        (-3.0 * cube + 3.0 * square + 3.0 * fraction + 1.0) / 6.0,
        cube / 6.0,
    )


def dense_tiles(geom, fraction, interval):
    knots = lax.broadcasted_iota(jnp.int32, (1, NK, 1), 1)
    tiles = jnp.zeros((geom.shape[0], NK, geom.shape[1]), jnp.float32)
    for offset, weight in enumerate(spline_weights(fraction)):
        hit = knots == (interval + offset)[:, None, :]
        tiles = tiles + jnp.where(hit, (geom * weight)[:, None, :], 0.0)
    return tiles


def block_layout(geom):
    tiles_all = geom.shape[1] // 128
    block = math.gcd(8, tiles_all)
    return (block, block * 128, tiles_all // block)


def block_tiles(geometry, fraction, interval, pattern, index, block, width):
    start = index * width
    geom = lax.dynamic_slice_in_dim(geometry, start, width, 1)
    frac = lax.dynamic_slice_in_dim(fraction, start, width, 1)
    knot = lax.dynamic_slice_in_dim(interval, start, width, 1)
    kinds = lax.dynamic_slice_in_dim(pattern, index * block, block, 1)
    tiles = dense_tiles(geom, frac, knot).reshape(geom.shape[0], NK, block, 128)
    return (tiles, kinds, start)


def forward(coeffs, geometry, fraction, interval, pattern):
    block, width, count = block_layout(geometry)

    def forward_step(index, image):
        tiles, kinds, start = block_tiles(
            geometry, fraction, interval, pattern, index, block, width
        )
        chosen = jnp.take(coeffs, kinds, axis=0)
        part = jnp.einsum("sktr,stk->tr", tiles, chosen, precision=lax.Precision.HIGHEST)
        return lax.dynamic_update_slice_in_dim(image, part.reshape(width), start, 0)

    return lax.fori_loop(0, count, forward_step, jnp.zeros((geometry.shape[1],), jnp.float32))


def backward(resid, per_coef, geometry, fraction, interval, pattern):
    block, width, count = block_layout(geometry)
    owners = lax.broadcasted_iota(jnp.int32, (1, 1, per_coef), 2)

    def backward_step(index, total):
        tiles, kinds, start = block_tiles(
            geometry, fraction, interval, pattern, index, block, width
        )
        piece = lax.dynamic_slice_in_dim(resid, start, width, 0).reshape(block, 128)
        contrib = jnp.einsum("sktr,tr->stk", tiles, piece, precision=lax.Precision.HIGHEST)
        picks = (kinds[:, :, None] == owners).astype(jnp.float32)
        return total + jnp.einsum("stc,stk->ck", picks, contrib, precision=lax.Precision.HIGHEST)

    return lax.fori_loop(0, count, backward_step, jnp.zeros((per_coef, NK), jnp.float32))


def on_device(geometry, fraction, interval, pattern, target):
    per_coef = TYPES // lax.axis_size("coef")

    def transpose_sum(resid):
        local = backward(resid, per_coef, geometry, fraction, interval, pattern).reshape(
            per_coef * NK
        )
        share = lax.psum(local, ("frame", "dom"))
        total = lax.psum(jnp.sum(share * share), "coef")
        return (share, total)

    def expand(share):
        return share.reshape(per_coef, NK)

    residual = target
    gradient, gamma = transpose_sum(residual)
    direction = gradient
    solution = jnp.zeros_like(gradient)
    for step_index in range(ITERS):
        partial_image = forward(expand(direction), geometry, fraction, interval, pattern)
        image = lax.psum(partial_image, "coef")
        image_total = lax.psum(jnp.sum(image * image), ("frame", "dom"))
        alpha = gamma / image_total
        solution = solution + alpha * direction
        residual = residual - alpha * image
        if step_index + 1 < ITERS:
            gradient, gamma_next = transpose_sum(residual)
            direction = gradient + gamma_next / gamma * direction
            gamma = gamma_next
    return (expand(solution), residual)


def solution(mesh):
    in_specs = (
        P("coef", ("frame", "dom")),
        P("coef", ("frame", "dom")),
        P("coef", ("frame", "dom")),
        P("coef", ("frame", "dom")),
        P(("frame", "dom")),
    )
    out_specs = (P("coef", None), P(("frame", "dom")))
    return jax.shard_map(
        on_device, mesh=mesh, in_specs=in_specs, out_specs=out_specs, check_vma=False
    )
```

profile of v0, /device:TPU:1, one launch (start us, length us, event | category | flops | bytes accessed | tf_op | source)
XLA Modules:
  0.0 1750.1 jit_solution(9884929640221820795)
XLA Ops:
  0.6 52.4 %while.56 = (s32[]{:T(128)}, f32[96,160]{0,1:T(8,128)S(1)}, s32[8,32]{1,0:T(8,128)}, f32[4096]{0:T(1024)}, s32[8,4096]{1,0:T(8,128)}, /*index=5*/f32[8,4096]{1,0...) while((s32[]{:T(128)}, f32[96,160]{0,1:T(8,128)S(1)}, ...), condition=%wide.region_1.2_spmd.clone, body=%wide.region_0.1_spmd.clone.sunk | while | flops 42192900 | bytes 11854863 | solution.py:75
  5.0 8.4 fusion.118
  18.1 8.4 fusion.118
  31.2 8.4 fusion.118
  44.3 8.4 fusion.118
  53.3 498.0 %psum.56 = f32[15360]{0:T(1024)S(1)} all-reduce(f32[15360]{0:T(1024)S(1)} %reshape.226), channel_id=1, replica_groups=mesh['frame'=16,'dom'=8,'coef'=4] {'frame','dom'}, use_global_device_ids=true, to_apply=%region_2.3 | all-reduce | flops 15360 | bytes 122880 | tf_op jit(solution)/shard_map/psum | solution.py:85
  551.4 53.3 %while.54 = (s32[]{:T(128)}, f32[4096]{0:T(1024)S(1)}, s32[8,4096]{1,0:T(8,128)}, f32[8,4096]{1,0:T(8,128)}, f32[8,4096]{1,0:T(8,128)}, /*index=5*/s32[8,32]{1,0...) while((s32[]{:T(128)}, f32[4096]{0:T(1024)S(1)}, ...), condition=%wide.region_6.0_spmd, body=%wide.region_5.7_spmd.sunk | while | flops 30371208 | bytes 11859845 | solution.py:59
  553.2 4.2 select_add_fusion.8
  558.3 6.1 fusion.108
  566.5 4.2 select_add_fusion.8
  571.6 6.1 fusion.108
  585.0 6.1 fusion.108
  598.3 6.1 fusion.108
  605.3 14.6 all-reduce
  620.5 256.4 %psum.59 = f32[]{:T(128)} all-reduce(f32[]{:T(128)} %multiply_reduce_fusion.3), channel_id=1, replica_groups=mesh['frame'=16,'dom'=8,'coef'=4] {'frame','dom'}, use_global_device_ids=true, to_apply=%region_9.11 | all-reduce | flops 1 | bytes 8 | tf_op jit(solution)/shard_map/psum | solution.py:99
  878.3 49.7 %while.57 = (s32[]{:T(128)}, f32[96,160]{0,1:T(8,128)S(1)}, s32[8,32]{1,0:T(8,128)}, f32[4096]{0:T(1024)S(1)}, s32[8,4096]{1,0:T(8,128)}, /*index=5*/f32[8,4096]...) while((s32[]{:T(128)}, f32[96,160]{0,1:T(8,128)S(1)}, ...), condition=%wide.region_11.13_spmd.clone, body=%wide.region_10.12_spmd.clone.sunk | while | flops 42192900 | bytes 11854863 | solution.py:75
  882.0 8.4 fusion.124
  894.4 8.4 fusion.124
  906.9 8.4 fusion.124
  919.3 8.4 fusion.124
  928.3 485.9 %psum.60 = f32[15360]{0:T(1024)S(1)} all-reduce(f32[15360]{0:T(1024)S(1)} %reshape.228), channel_id=1, replica_groups=mesh['frame'=16,'dom'=8,'coef'=4] {'frame','dom'}, use_global_device_ids=true, to_apply=%region_12.14 | all-reduce | flops 15360 | bytes 122880 | tf_op jit(solution)/shard_map/psum | solution.py:85
  1414.8 6.9 psum.61
  1423.1 53.3 %while.55 = (s32[]{:T(128)}, f32[4096]{0:T(1024)S(1)}, s32[8,4096]{1,0:T(8,128)}, f32[8,4096]{1,0:T(8,128)}, f32[8,4096]{1,0:T(8,128)}, /*index=5*/s32[8,32]{1,0...) while((s32[]{:T(128)}, f32[4096]{0:T(1024)S(1)}, ...), condition=%wide.region_16.18_spmd, body=%wide.region_15.17_spmd.sunk | while | flops 30371208 | bytes 11859845 | solution.py:59
  1424.8 4.2 select_add_fusion.9
  1430.0 6.1 fusion.113
  1443.3 6.1 fusion.113
  1451.5 4.2 select_add_fusion.9
  1456.6 6.1 fusion.113
  1464.8 4.2 select_add_fusion.9
  1470.0 6.1 fusion.113
  1476.4 12.1 psum.62
  1489.1 258.2 %psum.63 = f32[]{:T(128)} all-reduce(f32[]{:T(128)} %multiply_reduce_fusion.2), channel_id=1, replica_groups=mesh['frame'=16,'dom'=8,'coef'=4] {'frame','dom'}, use_global_device_ids=true, to_apply=%region_19.21 | all-reduce | flops 1 | bytes 8 | tf_op jit(solution)/shard_map/psum | solution.py:99
  (297 shorter events, 74.4 us)
Async XLA Ops:
  4.3 9.1 copy-start
  17.4 9.1 copy-start
  30.5 9.1 copy-start
  43.6 9.1 copy-start
  551.4 326.9 %copy-start.4 = (f32[4096]{0:T(1024)S(1)}, f32[4096]{0:T(1024)}, u32[]{:S(2)}) copy-start(f32[4096]{0:T(1024)} %get-tuple-element.1094) | copy-start | bytes 49156
  551.4 6.0 copy-start.1
  564.8 6.0 copy-start.1
  578.1 6.0 copy-start.1
  591.4 6.0 copy-start.1
  882.0 8.4 copy-start.2
  894.4 8.4 copy-start.2
  906.8 8.4 copy-start.2
  919.3 8.4 copy-start.2
  1423.1 6.0 copy-start.3
  1436.4 6.0 copy-start.3
  1449.8 6.0 copy-start.3
  1463.1 6.0 copy-start.3
where the time goes:
time: 1750 us
  blocking collectives  1530 us (87%)
  matrix products  118 us (7%)
  other arithmetic  78.9 us (5%)
    psum x2, blocking collectives, transpose_sum(): share = lax.psum(local, ('frame', 'dom'))  984 us
    psum x2, blocking collectives, on_device(): image_total = lax.psum(jnp.sum(image * image), ('frame', 'dom'))  515 us
    dot_general x8, matrix products, backward_step(): jnp.einsum('sktr,tr->stk', tiles, piece, precision=lax.Precision.HIGHEST)  66.9 us
    add x16, other arithmetic, dense_tiles(): tiles = tiles + jnp.where(hit, (geom * weight)[:, None, :], 0.0)  49.2 us
    dot_general x8, matrix products, forward_step(): jnp.einsum('sktr,stk->tr', tiles, chosen, precision=lax.Precision.HIGHEST)  49 us

commit v1 on v0

--- a/solution.py
+++ b/solution.py
@@ -7,6 +7,12 @@
 NK = 160
 TYPES = 384
 ITERS = 2
+
+
+def add_all(x, axis):
+    parts = lax.all_gather(x, axis, axis=0, tiled=False)
+    total = parts.sum(axis=0)
+    return total
 
 
 def spline_weights(fraction):
@@ -82,7 +88,7 @@
         local = backward(resid, per_coef, geometry, fraction, interval, pattern).reshape(
             per_coef * NK
         )
-        share = lax.psum(local, ("frame", "dom"))
+        share = add_all(local, ("frame", "dom"))
         total = lax.psum(jnp.sum(share * share), "coef")
         return (share, total)
 

time: 1750 us -> 1060 us (0.61)
  blocking collectives: 1530 us -> 538 us
  waiting for transfers between devices: 0 us -> 290 us
    psum x2 -> x0, blocking collectives: 984 us -> none  [transpose_sum(): share = lax.psum(local, ('frame', 'dom'))]
    all_gather x0 -> x2, waiting for transfers between devices: none -> 290 us  [add_all(): parts = lax.all_gather(x, axis, axis=0, tiled=False)]
  transfers between devices with their start and end apart: 0 -> 2, of which waited for: 0 -> 2; matrix products, arithmetic and copies ran while one was open for 0% -> 0% of each run, Pallas kernels for 0% -> 0%
where the time goes in v1:
time: 1060 us
  blocking collectives  538 us (51%)
  waiting for transfers between devices  290 us (27%)
  matrix products  118 us (11%)
  other arithmetic  73.3 us (7%)
  between operations  18.1 us (2%)
  local copies, waits for them, and re-layouts  15.5 us (1%)
    psum x2, blocking collectives, on_device(): image_total = lax.psum(jnp.sum(image * image), ('frame', 'dom'))  504 us
    all_gather x2, waiting for transfers between devices, add_all(): parts = lax.all_gather(x, axis, axis=0, tiled=False)  290 us
    dot_general x8, matrix products, backward_step(): jnp.einsum('sktr,tr->stk', tiles, piece, precision=lax.Precision.HIGHEST)  66.9 us
    add x16, other arithmetic, dense_tiles(): tiles = tiles + jnp.where(hit, (geom * weight)[:, None, :], 0.0)  49.2 us
    dot_general x8, matrix products, forward_step(): jnp.einsum('sktr,stk->tr', tiles, chosen, precision=lax.Precision.HIGHEST)  49 us
    psum x2, blocking collectives, on_device(): image = lax.psum(partial_image, 'coef')  25.2 us
  transfers between devices with their start and end apart: 2, of which 2 were waited for; matrix products, arithmetic and copies ran while one was open for 0% of the time, Pallas kernels for 0%

profile of v1, /device:TPU:1, one launch (start us, length us, event | category | flops | bytes accessed | tf_op | source)
XLA Modules:
  0.0 1055.5 jit_solution(6792258564208977422)
XLA Ops:
  7.2 52.4 %while.56 = (s32[]{:T(128)}, f32[96,160]{0,1:T(8,128)S(1)}, s32[8,32]{1,0:T(8,128)}, f32[4096]{0:T(1024)}, s32[8,4096]{1,0:T(8,128)}, /*index=5*/f32[8,4096]{1,0...) while((s32[]{:T(128)}, f32[96,160]{0,1:T(8,128)S(1)}, ...), condition=%wide.region_1.2_spmd.clone, body=%wide.region_0.1_spmd.clone.sunk | while | flops 42192900 | bytes 11854863 | solution.py:81
  11.6 8.4 fusion.118
  24.7 8.4 fusion.118
  37.8 8.4 fusion.118
  50.9 8.4 fusion.118
  60.8 151.3 %all-gather.5.cloned.1.call-done = f32[128,1,15360]{2,1,0:T(1,128)} async-done(((f32[1,1,15360]{2,1,0:T(1,128)}), f32[128,1,15360]{2,1,0:T(1,128)}) %all-gather.5.cloned.1.call-update) | async-done | bytes 7864336 | tf_op jit(solution)/shard_map/all_gather | solution.py:13
  212.1 6.4 reduce_sum.56
  219.2 47.1 %while.54 = (s32[]{:T(128)}, f32[4096]{0:T(1024)S(1)}, s32[8,4096]{1,0:T(8,128)S(1)}, f32[8,4096]{1,0:T(8,128)S(1)}, f32[8,4096]{1,0:T(8,128)S(1)}, /*index=5*/s...) while((s32[]{:T(128)}, f32[4096]{0:T(1024)S(1)}, ...), condition=%wide.region_6.0_spmd, body=%wide.region_5.7_spmd.sunk | while | flops 30371208 | bytes 11855721 | solution.py:65
  224.6 6.1 fusion.108
  236.4 6.1 fusion.108
  243.0 4.2 select_add_fusion.8
  248.2 6.1 fusion.108
  254.8 4.2 select_add_fusion.8
  260.0 6.1 fusion.108
  266.4 14.4 %all-reduce = (f32[4096]{0:T(1024)S(1)}, f32[]{:T(128)}) all-reduce(f32[4096]{0:T(1024)S(1)} %get-tuple-element.530, f32[]{:T(128)} %multiply_reduce_fusion.1), channel_id=1, replica_groups=mesh['frame'=16,'dom'=8,'coef'=4] {'coef'}, use_global_device_ids=true, to_apply=%region_7.9 | all-reduce | flops 4097 | bytes 32776 | tf_op jit(solution)/shard_map/psum | solution.py:104
  281.4 251.0 %psum.44 = f32[]{:T(128)} all-reduce(f32[]{:T(128)} %multiply_reduce_fusion.3), channel_id=1, replica_groups=mesh['frame'=16,'dom'=8,'coef'=4] {'frame','dom'}, use_global_device_ids=true, to_apply=%region_9.11 | all-reduce | flops 1 | bytes 8 | tf_op jit(solution)/shard_map/psum | solution.py:105
  533.8 43.6 %while.57 = (s32[]{:T(128)}, f32[96,160]{0,1:T(8,128)S(1)}, s32[8,32]{1,0:T(8,128)S(1)}, f32[4096]{0:T(1024)S(1)}, s32[8,4096]{1,0:T(8,128)S(1)}, /*index=5*/f32...) while((s32[]{:T(128)}, f32[96,160]{0,1:T(8,128)S(1)}, ...), condition=%wide.region_11.13_spmd.clone, body=%wide.region_10.12_spmd.clone.sunk | while | flops 42192900 | bytes 11850739 | solution.py:81
  535.9 8.4 fusion.124
  546.8 8.4 fusion.124
  557.7 8.4 fusion.124
  568.6 8.4 fusion.124
  578.2 138.8 %all-gather.7.cloned.1.call-done = f32[128,1,15360]{2,1,0:T(1,128)} async-done(((f32[1,1,15360]{2,1,0:T(1,128)}), f32[128,1,15360]{2,1,0:T(1,128)}) %all-gather.7.cloned.1.call-update) | async-done | bytes 7864336 | tf_op jit(solution)/shard_map/all_gather | solution.py:13
  717.1 6.4 reduce_sum.59
  724.2 9.4 psum.45
  734.9 47.1 %while.55 = (s32[]{:T(128)}, f32[4096]{0:T(1024)S(1)}, s32[8,4096]{1,0:T(8,128)S(1)}, f32[8,4096]{1,0:T(8,128)S(1)}, f32[8,4096]{1,0:T(8,128)S(1)}, /*index=5*/s...) while((s32[]{:T(128)}, f32[4096]{0:T(1024)S(1)}, ...), condition=%wide.region_16.18_spmd, body=%wide.region_15.17_spmd.sunk | while | flops 30371208 | bytes 11855721 | solution.py:65
  740.2 6.1 fusion.113
  752.0 6.1 fusion.113
  758.6 4.2 select_add_fusion.9
  763.8 6.1 fusion.113
  775.6 6.1 fusion.113
  782.0 10.8 %psum.46 = f32[4096]{0:T(1024)S(1)} all-reduce(f32[4096]{0:T(1024)S(1)} %get-tuple-element.532), channel_id=1, replica_groups=mesh['frame'=16,'dom'=8,'coef'=4] {'coef'}, use_global_device_ids=true, to_apply=%region_17.19 | all-reduce | flops 4096 | bytes 32768 | tf_op jit(solution)/shard_map/psum | solution.py:104
  793.4 252.5 %psum.47 = f32[]{:T(128)} all-reduce(f32[]{:T(128)} %multiply_reduce_fusion.2), channel_id=1, replica_groups=mesh['frame'=16,'dom'=8,'coef'=4] {'frame','dom'}, use_global_device_ids=true, to_apply=%region_19.21 | all-reduce | flops 1 | bytes 8 | tf_op jit(solution)/shard_map/psum | solution.py:105
  (286 shorter events, 66.0 us)
Async XLA Ops:
  7.2 205.0 %all-gather.5.cloned.1.call-start = ((), (), s32[]{:S(2)}) async-start(), calls=%async_computation | async-start | bytes 7925760 | tf_op jit(solution)/shard_map/all_gather | solution.py:13
  10.9 9.1 copy-start.3
  24.0 9.1 copy-start.3
  37.1 9.1 copy-start.3
  50.2 9.1 copy-start.3
  59.7 159.6 %copy-start = (s32[8,4096]{1,0:T(8,128)S(1)}, s32[8,4096]{1,0:T(8,128)}, u32[]{:S(2)}) copy-start(s32[8,4096]{1,0:T(8,128)} %get-tuple-element.1103) | copy-start | bytes 393220
  59.7 159.6 %copy-start.1 = (f32[8,4096]{1,0:T(8,128)S(1)}, f32[8,4096]{1,0:T(8,128)}, u32[]{:S(2)}) copy-start(f32[8,4096]{1,0:T(8,128)} %get-tuple-element.1106) | copy-start | bytes 393220
  59.7 159.5 %copy-start.2 = (f32[8,4096]{1,0:T(8,128)S(1)}, f32[8,4096]{1,0:T(8,128)}, u32[]{:S(2)}) copy-start(f32[8,4096]{1,0:T(8,128)} %get-tuple-element.1109) | copy-start | bytes 393220
  59.7 159.5 %copy-start.4 = (s32[8,32]{1,0:T(8,128)S(1)}, s32[8,32]{1,0:T(8,128)}, u32[]{:S(2)}) copy-start(s32[8,32]{1,0:T(8,128)} %get-tuple-element.1112) | copy-start | bytes 3076
  60.6 656.5 %all-gather.7.cloned.1.call-start = ((), (), s32[]{:S(2)}) async-start(), calls=%async_computation.1 | async-start | bytes 7925760 | tf_op jit(solution)/shard_map/all_gather | solution.py:13
  219.2 314.5 %copy-start.5 = (f32[4096]{0:T(1024)S(1)}, f32[4096]{0:T(1024)}, u32[]{:S(2)}) copy-start(f32[4096]{0:T(1024)} %get-tuple-element.1120) | copy-start | bytes 49156
Sparse Core Ops, SparseCore 0:
  60.7 151.3 all-gather.4
  578.4 138.6 all-gather.6
